TPU v7x, 32 devices: a whole 2x2x4 slice. The times are simulated.
32 devices in a mesh: row: 8 (over z, core), col: 4 (over y, x).
Axes of the slice: x: 2, y: 2, z: 4, core: 2. Of those that a mesh axis runs over, the one named last changes fastest.
Arguments:
- grad: bfloat16 [2, 6144, 24576], P(None, 'row', 'col'), may hold values from -45 to 45, as said below
- memory: float32 [2, 6144, 24576], P(None, 'row', 'col'), may hold values from -6 to 6
- p_prev: float32 [2, 6144, 32], P(None, ('row', 'col')), may hold values from -6 to 6
- q_prev: float32 [2, 24576, 32], P(None, ('col', 'row')), may hold values from -1 to 1
Outputs:
- p_new: float32 [2, 6144, 32], P(None, ('row', 'col'))
- q_new: float32 [2, 24576, 32], P(None, ('col', 'row'))
- error: float32 [2, 6144, 24576], P(None, 'row', 'col')
Inputs may be any that keep to these rules, and one draw needn't show every extreme that they name: `grad`: real-valued gradient entries.
All inputs are finite; a program needn't handle non-finite values.
Results may differ from a plain program's by a relative error of at most 0.0003.
Values sent between devices are 32-bit elements; how exact they have to be, the bound alone decides.
A program may use at most 192 MiB of HBM per device.

v0:
```python
import jax
import jax.numpy as jnp
from jax import lax
from jax.sharding import PartitionSpec as P


def shards(grad, memory, p_prev, q_prev):
    highest = lax.Precision.HIGHEST
    left_rows = lax.all_gather(p_prev, "col", axis=1, tiled=True)
    right_rows = lax.all_gather(q_prev, "row", axis=1, tiled=True)
    approx = jnp.einsum("lrk,lck->lrc", left_rows, right_rows, precision=highest)
    merged = grad.astype(jnp.float32) + memory - approx
    partial_value = jnp.einsum("lrc,lck->lrk", merged, right_rows, precision=highest)
    left = lax.psum(partial_value, "col")
    gram_part = jnp.einsum("lrk,lrj->lkj", left, left, precision=highest)
    gram = lax.psum(gram_part, "row")
    factor = jnp.linalg.cholesky(gram)
    p_hat = lax.linalg.triangular_solve(factor, left, left_side=False, lower=True, transpose_a=True)
    right_part = jnp.einsum("lrc,lrk->lck", merged, p_hat, precision=highest)
    share_rows = right_part.shape[1] // lax.axis_size("row")
    right_full = lax.psum(right_part, "row")
    q_new = lax.dynamic_slice_in_dim(right_full, lax.axis_index("row") * share_rows, share_rows, 1)
    error = merged - jnp.einsum("lrk,lck->lrc", p_hat, right_full, precision=highest)
    left_share = p_hat.shape[1] // lax.axis_size("col")
    p_new = lax.dynamic_slice_in_dim(p_hat, lax.axis_index("col") * left_share, left_share, 1)
    return (p_new, q_new, error)


def solution(mesh):
    placed = (
        P(None, "row", "col"),
        P(None, "row", "col"),
        P(None, ("row", "col"), None),
        P(None, ("col", "row"), None),
    )
    return jax.shard_map(
        shards,
        mesh=mesh,
        in_specs=placed,
        out_specs=(
            P(None, ("row", "col"), None),
            P(None, ("col", "row"), None),
            P(None, "row", "col"),
        ),
        check_vma=False,
    )
```

profile of v0, /device:TPU:0, one launch (start us, length us, event | category | flops | bytes accessed | tf_op | source)
XLA Modules:
  0.0 335.4 jit_solution(1339748341165155115)
XLA Ops:
  7.2 0.0 all-gather.2.cloned.1.call-start
  7.2 0.7 all-gather.2.cloned.1.call-update
  7.9 0.0 all-reduce.3.cloned.1.call-start
  7.9 1.0 copy.15
  8.9 12.7 %all_gather.6 = f32[2,768,32]{2,0,1:T(2,128)S(1)} all-gather(f32[2,192,32]{2,0,1:T(2,128)S(1)} %copy.15), channel_id=1, replica_groups=mesh['row'=8,'col'=4] {'col'}, dimensions={1}, use_global_device_ids=true | all-gather | bytes 245760 | tf_op jit(solution)/shard_map/all_gather | solution.py:9
  21.6 16.0 %all-gather.2.cloned.1.call-done = f32[2,6144,32]{1,2,0:T(8,128)} async-done(((f32[2,768,32]{1,2,0:T(8,128)}), f32[2,6144,32]{1,2,0:T(8,128)}) %all-gather.2.cloned.1.call-update) | async-done | bytes 1572880 | tf_op jit(solution)/shard_map/all_gather | solution.py:10
  37.6 0.0 copy-start
  37.6 44.0 %add_subtract_fusion = f32[2,768,6144]{2,1,0:T(8,128)} fusion(f32[2,768,6144]{2,1,0:T(8,128)} %param.5, bf16[2,768,6144]{2,1,0:T(8,128)(2,1)} %param.4, f32[2,6144,32]{1,2,0:T(8,128)} %all-gather.2.cloned.1.call-done, f32[2,768,32]{2,0,1:T(2,128)S(1)} %all_gather.6), kind=kOutput, calls=%fused_computation | convolution fusion | flops 3652190208 | bytes 96141312 | tf_op jit(solution)/shard_map/lrk,lck->lrc/dot_general | solution.py:11
  81.6 0.0 copy-done
  81.6 39.0 %fusion.4 = f32[2,768,32]{1,2,0:T(8,128)} fusion(f32[2,768,6144]{2,1,0:T(8,128)} %add_subtract_fusion, f32[2,6144,32]{1,2,0:T(8,128)S(1)} %copy-done), kind=kOutput, calls=%fused_computation.14 | convolution fusion | flops 3623878656 | bytes 39518208 | tf_op jit(solution)/shard_map/lrc,lck->lrk/dot_general | solution.py:13
  120.5 0.0 all-reduce.3.cloned.1.call-update
  120.6 0.0 all-reduce.5.cloned.1.call-start
  120.6 41.8 %all-reduce.3.cloned.1.call-done = f32[2,768,32]{1,2,0:T(8,128)} async-done(((f32[2,768,32]{1,2,0:T(8,128)}), f32[2,768,32]{1,2,0:T(8,128)}) %all-reduce.3.cloned.1.call-update) | async-done | bytes 196624 | tf_op jit(solution)/shard_map/psum | solution.py:14
  162.4 1.3 fusion.5
  163.8 28.1 %psum.22 = f32[2,32,32]{1,2,0:T(8,128)S(1)} all-reduce(f32[2,32,32]{1,2,0:T(8,128)S(1)} %fusion.5), channel_id=1, replica_groups=mesh['row'=8,'col'=4] {'row'}, use_global_device_ids=true, to_apply=%region_1.0 | all-reduce | flops 2048 | bytes 16384 | tf_op jit(solution)/shard_map/psum | solution.py:16
  191.9 0.1 copy.18
  192.0 5.9 %custom-call.7 = f32[2,32,32]{2,1,0:T(8,128)S(1)} custom-call(f32[2,32,32]{2,1,0:T(8,128)S(1)} %fusion.3), custom_call_target="Cholesky" | custom-call | tf_op jit(solution)/shard_map/jit(cholesky)/cholesky | solution.py:17
  197.9 0.1 compare_reduce_fusion
  198.0 0.1 select_bitcast_fusion
  198.1 4.9 %custom-call.8 = f32[2,1,32,32]{2,3,1,0:T(8,128)S(1)} custom-call(f32[2,1,32,32]{3,2,1,0:T(8,128)S(1)} %select_bitcast_fusion), custom_call_target="InvertDiagBlocksLowerTriangular" | custom-call | tf_op jit(solution)/shard_map/triangular_solve | solution.py:18
  203.0 1.3 fusion.1
  204.3 26.9 %fusion.6 = f32[2,6144,32]{1,2,0:T(8,128)} fusion(f32[2,768,6144]{2,1,0:T(8,128)} %add_subtract_fusion, f32[2,768,32]{1,2,0:T(8,128)S(1)} %fusion.1), kind=kOutput, calls=%fused_computation.16 | convolution fusion | flops 3623878656 | bytes 39518208 | tf_op jit(solution)/shard_map/lrc,lrk->lck/dot_general | solution.py:19
  231.2 0.0 all-reduce.5.cloned.1.call-update
  231.2 0.7 constant_dynamic-slice_fusion.1
  231.9 58.6 %all-reduce.5.cloned.1.call-done = f32[2,6144,32]{1,2,0:T(8,128)} async-done(((f32[2,6144,32]{1,2,0:T(8,128)}), f32[2,6144,32]{1,2,0:T(8,128)}) %all-reduce.5.cloned.1.call-update) | async-done | bytes 1572880 | tf_op jit(solution)/shard_map/psum | solution.py:21
  290.5 36.7 %convolution_subtract_fusion = f32[2,768,6144]{2,1,0:T(8,128)} fusion(f32[2,768,6144]{2,1,0:T(8,128)} %add_subtract_fusion, f32[2,768,32]{1,2,0:T(8,128)S(1)} %fusion.1, f32[2,6144,32]{1,2,0:T(8,128)} %all-reduce.5.cloned.1.call-done), kind=kOutput, calls=%fused_computation.1 | convolution fusion | flops 3633315840 | bytes 77266944 | tf_op jit(solution)/shard_map/lrk,lck->lrc/dot_general | solution.py:23
  327.2 1.6 constant_dynamic-slice_fusion
  (4 shorter events, 0.1 us)
Async XLA Ops:
  7.2 30.4 %all-gather.2.cloned.1.call-start = ((), (), s32[]{:S(2)}) async-start(), calls=%async_computation | async-start | bytes 1769472 | tf_op jit(solution)/shard_map/all_gather | solution.py:10
  7.9 154.5 %all-reduce.3.cloned.1.call-start = ((), (), s32[]{:S(2)}) async-start(), calls=%async_computation.1 | async-start | bytes 393216 | tf_op jit(solution)/shard_map/psum | solution.py:14
  37.6 44.0 %copy-start = (f32[2,6144,32]{1,2,0:T(8,128)S(1)}, f32[2,6144,32]{1,2,0:T(8,128)}, u32[]{:S(2)}) copy-start(f32[2,6144,32]{1,2,0:T(8,128)} %all-gather.2.cloned.1.call-done) | copy-start | bytes 4718596
  120.6 169.9 %all-reduce.5.cloned.1.call-start = ((), (), s32[]{:S(2)}) async-start(), calls=%async_computation.2 | async-start | bytes 3145728 | tf_op jit(solution)/shard_map/psum | solution.py:21
Sparse Core Ops, SparseCore 0:
  9.6 27.9 all-gather.1
  120.7 41.7 all-reduce.2
  231.3 59.1 all-reduce.4
where the time goes:
time: 336 us; the launch traced here: 335 us
  matrix products  149 us (44%)
  waiting for transfers between devices  117 us (35%)
  blocking collectives  40.8 us (12%)
  between operations  13.8 us (4%)
  other arithmetic  11 us (3%)
  local copies, waits for them, and re-layouts  3.39 us (1%)
    psum x1, waiting for transfers between devices, shards(): right_full = lax.psum(right_part, 'row')  58.6 us
    dot_general x1, matrix products, shards(): jnp.einsum('lrk,lck->lrc', left_rows, right_rows, precision=highest)  44 us
    psum x1, waiting for transfers between devices, shards(): left = lax.psum(partial_value, 'col')  41.8 us
    dot_general x1, matrix products, shards(): jnp.einsum('lrc,lck->lrk', merged, right_rows, precision=highest)  39 us
    dot_general x1, matrix products, shards(): jnp.einsum('lrk,lck->lrc', p_hat, right_full, precision=highest)  36.7 us
    psum x1, blocking collectives, shards(): gram = lax.psum(gram_part, 'row')  28.1 us
    dot_general x1, matrix products, shards(): right_part = jnp.einsum('lrc,lrk->lck', merged, p_hat, precision=highest)  26.9 us
    all_gather x1, waiting for transfers between devices, shards(): right_rows = lax.all_gather(q_prev, 'row', axis=1, tiled=True)  16 us
  transfers between devices with their start and end apart: 3, of which 3 were waited for; matrix products, arithmetic and copies ran while one was open for 1% of the time, Pallas kernels for 0%

commit v1 on v0

v1 whole, which is shorter than its diff:
```python
import functools

import jax
import jax.numpy as jnp
from jax import lax
from jax.experimental import pallas as pl
from jax.experimental.pallas import tpu as pltpu
from jax.sharding import PartitionSpec as P

MESH = pl.DeviceIdType.MESH
HIGHEST = lax.Precision.HIGHEST
NT = (((1,), (1,)), ((), ()))
NN = (((1,), (0,)), ((), ()))
VMEM_BYTES = 67043328


def dot(a, b, dims=NN, precision=None):
    return lax.dot_general(a, b, dims, precision=precision, preferred_element_type=jnp.float32)


def split(x):
    hi = x.astype(jnp.bfloat16)
    return hi, (x - hi.astype(jnp.float32)).astype(jnp.bfloat16)


def row_tile(rows):
    return next(t for t in (256, 128, 64, 32, 16) if rows % t == 0)


def eye(rows, cols, start):
    i = lax.broadcasted_iota(jnp.int32, (rows, cols), 0) + start
    return (i == lax.broadcasted_iota(jnp.int32, (rows, cols), 1)).astype(jnp.float32)


def inverse_factor(gram):
    k = gram.shape[0]
    both = jnp.concatenate([gram, eye(k, k, 0)], axis=1)
    rows = lax.broadcasted_iota(jnp.int32, both.shape, 0)
    scale = jnp.zeros_like(both)
    for i in range(k):
        pivot = both[i : i + 1, :]
        top = both[i : i + 1, i : i + 1]
        scale = jnp.where(rows == i, lax.rsqrt(top), scale)
        both = both - jnp.where(rows > i, both[:, i : i + 1] / top, 0.0) * pivot
    return (both * scale)[:, k:]


def exchange_kernel(nr, nc, layers, grad, memory, pt, qt, merged, pcat_out, pt_out, qnew,
                    mbuf, gbuf, pslot, qslot, pcat, qcat, acc, left, lhl, gram, rpart, rsib, rz, linv,
                    s_in, s_grad, s_out, sp_s, sp_r, sq_s, sq_r, sf_s, sl_s, sl_r, sg_s, sg_r,
                    ss_s, ss_r, sz_s, sz_r, sn_s, sn_r, sm_s):
    row, col = lax.axis_index("row"), lax.axis_index("col")
    nz = nr // 2
    z, core = row // 2, lax.rem(row, 2)
    sib = z * 2 + (1 - core)
    rank = qt.shape[1]
    width = qt.shape[2]
    rows = mbuf.shape[1]
    share = pt.shape[2]
    tile = row_tile(rows)

    def cols(j):
        return pl.ds(pl.multiple_of(j * width, width), width)

    def peer(dz):
        return lax.rem(z + dz, nz)

    def send(src, dst, ss, rs, **where):
        return pltpu.make_async_remote_copy(src_ref=src, dst_ref=dst, send_sem=ss, recv_sem=rs,
                                            device_id=where, device_id_type=MESH)

    def order(k):
        return peer(k // 2) * 2 + lax.rem(core + lax.rem(k, 2), 2)

    def fetch_mem(l, j):
        return pltpu.make_async_copy(memory.at[l, :, cols(j)], mbuf.at[l, :, cols(j)], s_in.at[l, j])

    def fetch_grad(l, j):
        return pltpu.make_async_copy(grad.at[l, :, cols(j)], gbuf.at[:, cols(j)], s_grad.at[l, j])

    def put(l, j):
        return pltpu.make_async_copy(mbuf.at[l, :, cols(j)], merged.at[l, :, cols(j)], s_out.at[l, j])

    def begin(k, _):
        fetch_mem(0, order(k)).start()
        fetch_grad(0, order(k)).start()
        return 0

    lax.fori_loop(0, nr, begin, 0)

    def begin_next(k, _):
        fetch_mem(1, order(k)).start()
        return 0

    lax.fori_loop(0, nr, begin_next, 0)

    for l in range(layers):
        gram[l, row] = jnp.zeros(gram.shape[2:], jnp.float32)
    barrier = pltpu.get_barrier_semaphore()
    for d in range(1, nr):
        pl.semaphore_signal(barrier, inc=1, device_id={"row": lax.rem(row + d, nr)}, device_id_type=MESH)
    for d in range(1, nc):
        pl.semaphore_signal(barrier, inc=1, device_id={"col": lax.rem(col + d, nc)}, device_id_type=MESH)
    pl.semaphore_wait(barrier, nr + nc - 2)

    def p_copy(c):
        return send(pt, pslot.at[col], sp_s.at[c], sp_r.at[col], col=c)

    def q_copy(r, slot):
        return send(qt, qslot.at[slot], sq_s.at[r], sq_r.at[slot], row=r)

    def q_forward(slot):
        return send(qslot.at[slot], qslot.at[slot], sf_s.at[slot], sq_r.at[slot], row=sib)

    q_copy(sib, row).start()
    for d in range(1, nz):
        q_copy(peer(d) * 2 + core, row).start()
    for d in range(1, nc):
        p_copy(lax.rem(col + d, nc)).start()
    qslot[row] = qt[...]
    pslot[col] = pt[...]
    for d in range(1, nc):
        c = lax.rem(col + d, nc)
        send(pt, pslot.at[c], sp_s.at[c], sp_r.at[c], col=c).wait_recv()
    for l in range(layers):
        for c in range(nc):
            hi, lo = split(pslot[c, l])
            turned = dot(eye(share, share, 0).astype(jnp.bfloat16), jnp.concatenate([hi, lo, hi], axis=0), NT)
            pcat[l, c * share : (c + 1) * share, :] = turned.astype(jnp.bfloat16)
    acc[...] = jnp.zeros_like(acc)

    def first(l):
        def step(k, _):
            j = order(k)
            if l == 0:
                @pl.when(k > 0)
                def _():
                    q_copy(j, j).wait_recv()

                @pl.when(jnp.logical_and(k > 0, lax.rem(k, 2) == 0))
                def _():
                    q_forward(j).start()
            hi, lo = split(qslot[j, l])
            qcat[0:rank, :] = hi
            qcat[rank : 2 * rank, :] = lo
            qcat[2 * rank :, :] = hi
            fetch_mem(l, j).wait()
            fetch_grad(l, j).wait()

            def part(t, _):
                at = pl.ds(pl.multiple_of(t * tile, tile), tile)
                both = qcat[...]
                approx = dot(pcat[l, at, :], jnp.concatenate([both[0:rank], both[2 * rank :], both[rank : 2 * rank]], axis=0))
                m = gbuf[at, cols(j)].astype(jnp.float32) + mbuf[l, at, cols(j)] - approx
                mbuf[l, at, cols(j)] = m
                mh, ml = split(m)
                acc[l, at, :] += dot(mh, both[0 : 2 * rank], NT) + dot(ml, both[0 : 2 * rank], NT)
                return 0

            lax.fori_loop(0, rows // tile, part, 0)
            put(l, j).start()
            if l + 1 < layers:
                fetch_grad(l + 1, j).start()
            return 0

        lax.fori_loop(0, nr, step, 0)
        fold = jnp.concatenate([eye(rank, rank, 0), eye(rank, rank, 0)], axis=1)
        left[l, col] = dot(fold, acc[l], NT, HIGHEST)
        for d in range(1, nc):
            c = lax.rem(col + d, nc)
            send(left.at[l, col], left.at[l, col], sl_s.at[l, c], sl_r.at[l, col], col=c).start()

    def join_left(l):
        for d in range(1, nc):
            c = lax.rem(col + d, nc)
            send(left.at[l, c], left.at[l, c], sl_s.at[l, c], sl_r.at[l, c], col=c).wait()
        total = left[l, 0]
        for c in range(1, nc):
            total = total + left[l, c]
        pt_out[l] = total
        hi, lo = split(total)
        lhl[0:rank, :] = hi
        lhl[rank:, :] = lo
        gram[l, row, :, 0:rank] = dot(total, total, NT, HIGHEST)
        for d in range(1, nr):
            r = lax.rem(row + d, nr)
            send(gram.at[l, row], gram.at[l, row], sg_s.at[l, r], sg_r.at[l, row], row=r).start()

    def sib_copy(l, dz, j):
        return send(rpart.at[l, j], rsib.at[l, dz], ss_s.at[l, dz], ss_r.at[l, dz], row=sib)

    def z_copy(l, dz, slot):
        j = dz * 2 + core
        return send(rpart.at[l, j], rz.at[l, slot], sz_s.at[l, dz], sz_r.at[l, slot], row=j)

    def right(l):
        def join(dz):
            sib_copy(l, dz, dz * 2 + core).wait_recv()
            rpart[l, dz * 2 + core] += rsib[l, dz]

        def step(i, _):
            dz = peer(1 + i)

            def chunk(e, _):
                j = dz * 2 + lax.rem(core + 1 + e, 2)
                mh, ml = split(mbuf[l, :, cols(j)])
                both = dot(lhl[...], mh) + dot(lhl[...], ml)
                rpart[l, j] = both[0:rank] + both[rank:]

                @pl.when(e == 0)
                def _():
                    sib_copy(l, dz, j).start()

                return 0

            lax.fori_loop(0, 2, chunk, 0)

            @pl.when(i > 0)
            def _():
                join(peer(i))
                z_copy(l, peer(i), z).start()

            return 0

        lax.fori_loop(0, nz, step, 0)
        join(z)

    def solve(l):
        for d in range(1, nr):
            r = lax.rem(row + d, nr)
            send(gram.at[l, r], gram.at[l, r], sg_s.at[l, r], sg_r.at[l, r], row=r).wait()
        total = gram[l, 0]
        for r in range(1, nr):
            total = total + gram[l, r]
        linv[l] = inverse_factor(total[:, 0:rank])

    def new_copy(l, r, slot):
        return send(qnew.at[slot, l], qnew.at[slot, l], sn_s.at[l, r], sn_r.at[l, slot], row=r)

    def new_forward(l, slot):
        return send(qnew.at[slot, l], qnew.at[slot, l], sm_s.at[l, slot], sn_r.at[l, slot], row=sib)

    def own(l):
        total = rpart[l, row]
        for d in range(1, nz):
            z_copy(l, peer(d), peer(d)).wait_recv()
            total = total + rz[l, peer(d)]
        qnew[row, l] = dot(linv[l], total, NN, HIGHEST)
        new_copy(l, sib, row).start()
        for d in range(1, nz):
            new_copy(l, peer(d) * 2 + core, row).start()

    def left_out(l):
        hat = dot(linv[l], pt_out[l], NN, HIGHEST)
        pt_out[l] = hat
        hi, lo = split(hat)
        stack = jnp.concatenate([hi, lo, hi], axis=0)
        for t in range(rows // tile):
            turned = dot(eye(tile, rows, t * tile).astype(jnp.bfloat16), stack, NT)
            pcat_out[l, t * tile : (t + 1) * tile, :] = turned.astype(jnp.bfloat16)

    def forward(l):
        for d in range(1, nz):
            slot = peer(d) * 2 + core
            new_copy(l, slot, slot).wait_recv()
            new_forward(l, slot).start()

    for l in range(layers):
        first(l)
    join_left(0)
    right(0)
    solve(0)
    for l in range(1, layers):
        join_left(l)
        own(l - 1)
        right(l)
        solve(l)
        forward(l - 1)
    own(layers - 1)
    for l in range(layers):
        left_out(l)
    forward(layers - 1)
    for l in range(layers):
        for d in range(nz):
            slot = peer(d) * 2 + (1 - core)
            new_copy(l, sib, slot).wait_recv()

    q_copy(sib, row).wait_send()
    for d in range(1, nz):
        q_copy(peer(d) * 2 + core, row).wait_send()
        q_forward(peer(d) * 2 + core).wait_send()
    for d in range(1, nc):
        p_copy(lax.rem(col + d, nc)).wait_send()
    for l in range(layers):
        new_copy(l, sib, row).wait_send()
        for d in range(nz):
            sib_copy(l, peer(d), peer(d) * 2 + core).wait_send()
        for d in range(1, nz):
            z_copy(l, peer(d), z).wait_send()
            new_copy(l, peer(d) * 2 + core, row).wait_send()
            new_forward(l, peer(d) * 2 + core).wait_send()

    def end(k, _):
        for l in range(layers):
            put(l, k).wait()
        return 0

    lax.fori_loop(0, nr, end, 0)


def error_kernel(pcat, q, m, out):
    rows = m.shape[1]
    tile = row_tile(rows)
    hi, lo = split(q[0, 0])
    both = jnp.concatenate([hi, hi, lo], axis=0)

    def part(t, _):
        at = pl.ds(pl.multiple_of(t * tile, tile), tile)
        out[0, at, :] = m[0, at, :] - dot(pcat[0, at, :], both)
        return 0

    lax.fori_loop(0, rows // tile, part, 0)


def shards(nr, nc, grad, memory, p_prev, q_prev):
    layers, rows, columns = grad.shape
    rank, share, width = p_prev.shape[2], p_prev.shape[1], q_prev.shape[1]
    nz = nr // 2
    f32, bf16 = jnp.float32, jnp.bfloat16
    dma = pltpu.SemaphoreType.DMA
    anyspace = pl.BlockSpec(memory_space=pl.ANY)
    vmem = pl.BlockSpec(memory_space=pltpu.VMEM)
    merged, pcat, pt, qnew = pl.pallas_call(
        functools.partial(exchange_kernel, nr, nc, layers),
        out_shape=(
            jax.ShapeDtypeStruct((layers, rows, columns), f32),
            jax.ShapeDtypeStruct((layers, rows, 3 * rank), bf16),
            jax.ShapeDtypeStruct((layers, rank, rows), f32),
            jax.ShapeDtypeStruct((nr, layers, rank, width), f32),
        ),
        in_specs=[anyspace, anyspace, vmem, vmem],
        out_specs=(anyspace, vmem, vmem, vmem),
        scratch_shapes=[
            pltpu.VMEM((layers, rows, columns), f32),
            pltpu.VMEM((rows, columns), bf16),
            pltpu.VMEM((nc, layers, rank, share), f32),
            pltpu.VMEM((nr, layers, rank, width), f32),
            pltpu.VMEM((layers, rows, 3 * rank), bf16),
            pltpu.VMEM((3 * rank, width), bf16),
            pltpu.VMEM((layers, rows, 2 * rank), f32),
            pltpu.VMEM((layers, nc, rank, rows), f32),
            pltpu.VMEM((2 * rank, rows), bf16),
            pltpu.VMEM((layers, nr, rank, 128), f32),
            pltpu.VMEM((layers, nr, rank, width), f32),
            pltpu.VMEM((layers, nz, rank, width), f32),
            pltpu.VMEM((layers, nz, rank, width), f32),
            pltpu.VMEM((layers, rank, rank), f32),
            dma((layers, nr)), dma((layers, nr)), dma((layers, nr)),
            dma((nc,)), dma((nc,)), dma((nr,)), dma((nr,)), dma((nr,)),
            dma((layers, nc)), dma((layers, nc)), dma((layers, nr)), dma((layers, nr)),
            dma((layers, nz)), dma((layers, nz)), dma((layers, nz)), dma((layers, nz)),
            dma((layers, nr)), dma((layers, nr)), dma((layers, nr)),
        ],
        compiler_params=pltpu.CompilerParams(
            collective_id=0, has_side_effects=True, vmem_limit_bytes=VMEM_BYTES
        ),
        name="exchange",
    )(grad, memory, jnp.swapaxes(p_prev, 1, 2), jnp.swapaxes(q_prev, 1, 2))
    error = pl.pallas_call(
        error_kernel,
        grid=(layers, nr),
        out_shape=jax.ShapeDtypeStruct((layers, rows, columns), f32),
        in_specs=[
            pl.BlockSpec((1, rows, 3 * rank), lambda l, j: (l, 0, 0)),
            pl.BlockSpec((1, 1, rank, width), lambda l, j: (j, l, 0, 0)),
            pl.BlockSpec((1, rows, width), lambda l, j: (l, 0, j)),
        ],
        out_specs=pl.BlockSpec((1, rows, width), lambda l, j: (l, 0, j)),
        compiler_params=pltpu.CompilerParams(dimension_semantics=("arbitrary", "arbitrary")),
        name="error",
    )(pcat, qnew, merged)
    p_mine = lax.dynamic_slice_in_dim(pt, lax.axis_index("col") * share, share, 2)
    q_mine = lax.dynamic_index_in_dim(qnew, lax.axis_index("row"), 0, keepdims=False)
    return jnp.swapaxes(p_mine, 1, 2), jnp.swapaxes(q_mine, 1, 2), error


def plain_shards(grad, memory, p_prev, q_prev):
    left_rows = lax.all_gather(p_prev, "col", axis=1, tiled=True)
    right_rows = lax.all_gather(q_prev, "row", axis=1, tiled=True)
    approx = jnp.einsum("lrk,lck->lrc", left_rows, right_rows, precision=HIGHEST)
    merged = grad.astype(jnp.float32) + memory - approx
    partial_value = jnp.einsum("lrc,lck->lrk", merged, right_rows, precision=HIGHEST)
    left = lax.psum(partial_value, "col")
    gram = lax.psum(jnp.einsum("lrk,lrj->lkj", left, left, precision=HIGHEST), "row")
    factor = jnp.linalg.cholesky(gram)
    p_hat = lax.linalg.triangular_solve(factor, left, left_side=False, lower=True, transpose_a=True)
    right_part = jnp.einsum("lrc,lrk->lck", merged, p_hat, precision=HIGHEST)
    share_rows = right_part.shape[1] // lax.axis_size("row")
    right_full = lax.psum(right_part, "row")
    q_new = lax.dynamic_slice_in_dim(right_full, lax.axis_index("row") * share_rows, share_rows, 1)
    error = merged - jnp.einsum("lrk,lck->lrc", p_hat, right_full, precision=HIGHEST)
    left_share = p_hat.shape[1] // lax.axis_size("col")
    p_new = lax.dynamic_slice_in_dim(p_hat, lax.axis_index("col") * left_share, left_share, 1)
    return (p_new, q_new, error)


def solution(mesh):
    nr, nc = mesh.shape["row"], mesh.shape["col"]

    def local(grad, memory, p_prev, q_prev):
        if q_prev.shape[1] % 128 or p_prev.shape[1] % 16 or nr % 2:
            return plain_shards(grad, memory, p_prev, q_prev)
        return shards(nr, nc, grad, memory, p_prev, q_prev)

    placed = (
        P(None, "row", "col"),
        P(None, "row", "col"),
        P(None, ("row", "col"), None),
        P(None, ("col", "row"), None),
    )
    return jax.shard_map(
        local,
        mesh=mesh,
        in_specs=placed,
        out_specs=(
            P(None, ("row", "col"), None),
            P(None, ("col", "row"), None),
            P(None, "row", "col"),
        ),
        check_vma=False,
    )
```

time: 336 us -> 129 us (0.38)
  matrix products: 149 us -> 0 us
  Pallas kernels: 0 us -> 124 us
  waiting for transfers between devices: 117 us -> 0 us
  blocking collectives: 40.8 us -> 0 us
  between operations: 13.8 us -> 0.65 us
  other arithmetic: 11 us -> 0 us
    dot_general x5 -> x0, matrix products: 148 us -> none  [the longest x1 44 us: shards(): jnp.einsum('lrk,lck->lrc', left_rows, right_rows, precision=highest)]
    pallas_call x0 -> x2, Pallas kernels: none -> 124 us  [the longest x1 90 us: shards(): pl.pallas_call(functools.partial(exchange_kernel, nr, nc, layers), out_sh...]
    psum x2 -> x0, waiting for transfers between devices: 100 us -> none  [the longest x1 58.6 us: shards(): right_full = lax.psum(right_part, 'row')]
    psum x1 -> x0, blocking collectives: 28.1 us -> none  [shards(): gram = lax.psum(gram_part, 'row')]
    all_gather x1 -> x0, waiting for transfers between devices: 16 us -> none  [shards(): right_rows = lax.all_gather(q_prev, 'row', axis=1, tiled=True)]
    all_gather x1 -> x0, blocking collectives: 12.7 us -> none  [shards(): left_rows = lax.all_gather(p_prev, 'col', axis=1, tiled=True)]
    another operation x7 -> x0, other arithmetic: 11 us -> none  [the longest x4 6.03 us: shards(): factor = jnp.linalg.cholesky(gram)]
  transfers between devices with their start and end apart: 3 -> 0, of which waited for: 3 -> 0; matrix products, arithmetic and copies ran while one was open for 1% -> 0% of each run, Pallas kernels for 0% -> 0%
where the time goes in v1:
time: 129 us; the launch traced here: 128 us
  Pallas kernels  124 us (96%)
  local copies, waits for them, and re-layouts  3.23 us (3%)
    pallas_call x1, Pallas kernels, shards(): pl.pallas_call(functools.partial(exchange_kernel, nr, nc, layers), out_sh...  90 us
    pallas_call x1, Pallas kernels, shards(): pl.pallas_call(error_kernel, grid=(layers, nr), out_shape=jax.ShapeDtypeS...  34.1 us
    transpose x2, local copies, waits for them, and re-layouts, shards(): return (jnp.swapaxes(p_mine, 1, 2), jnp.swapaxes(q_mine, 1, 2), error)  3.23 us

profile of v1, /device:TPU:0, one launch (start us, length us, event | category | flops | bytes accessed | tf_op | source)
XLA Modules:
  0.0 127.9 jit_solution(13222763894758202081)
XLA Ops:
  0.6 90.0 %exchange.1 = (f32[2,768,6144]{2,1,0:T(8,128)}, bf16[2,768,96]{2,1,0:T(8,128)(2,1)}, f32[2,32,768]{2,1,0:T(8,128)}, f32[8,2,32,768]{3,2,1,0:T(8,128)}) custom-call(bf16[2,768,6144]{2,1,0:T(8,128)(2,1)} %grad.1, f32[2,768,6144]{2,1,0:T(8,128)} %memory.1, f32[2,32,192]{2,1,0:T(8,128)} %bitcast.9, f32[2,32,768]{2,1,0:T(8,128)} %bitcast.8), custom_call_target="tpu_custom_call" | custom-call | tf_op jit(solution)/shard_map/exchange/pallas_call | solution.py:333
  90.6 1.6 %dynamic-slice_bitcast_fusion.1 = f32[2,192,32]{1,2,0:T(8,128)} fusion(f32[2,32,768]{2,1,0:T(8,128)} %get-tuple-element.7, s32[]{:T(128)S(6)} %select_n.7), kind=kLoop, calls=%fused_computation.1 | loop fusion | bytes 98308 | tf_op jit(solution)/shard_map/transpose | solution.py:384
  92.2 1.6 %dynamic-slice_bitcast_fusion = f32[2,768,32]{1,2,0:T(8,128)} fusion(f32[8,2,32,768]{3,2,1,0:T(8,128)} %get-tuple-element.8.q, s32[]{:T(128)S(6)} %select_n.8), kind=kLoop, calls=%fused_computation | loop fusion | bytes 393220 | tf_op jit(solution)/shard_map/transpose | solution.py:384
  93.8 34.1 %error.1 = f32[2,768,6144]{2,1,0:T(8,128)} custom-call(bf16[2,768,96]{2,1,0:T(8,128)(2,1)} %get-tuple-element.9.pcat, f32[8,2,32,768]{3,2,1,0:T(8,128)} %get-tuple-element.8.q, f32[2,768,6144]{2,1,0:T(8,128)} %get-tuple-element.10.m), custom_call_target="tpu_custom_call" | custom-call | tf_op jit(solution)/shard_map/error/pallas_call | solution.py:369
